TPU v7x, 32 devices: a whole 2x2x4 slice. The times are simulated.
32 devices in a mesh: row: 8 (over y, x, core), rep: 4 (over z).
Axes of the slice: x: 2, y: 2, z: 4, core: 2. Of those that a mesh axis runs over, the one named last changes fastest.
Arguments:
- features: bfloat16 [8192, 256], P('row'), may hold values from -6 to 6
- weight_self: bfloat16 [256, 256], replicated, may hold values from -0.375 to 0.375
- weight_neigh: bfloat16 [256, 256], replicated, may hold values from -0.375 to 0.375
- degrees: int32 [8192], P('row'), may hold values from 1 to 47
- tile_values: bfloat16 [8, 8, 48, 128, 128], P('row', 'rep'), may hold values from 0 to 1
- tile_blocks: int32 [8, 8, 48, 2], P('row', 'rep'), may hold values from 0 to 7
- tile_count: int32 [8, 8], P('row', 'rep'), may hold values from 1 to 48, as said below
- cotangent: bfloat16 [8192, 256], P(('row', 'rep')), may hold values from -6 to 6
Outputs:
- output: bfloat16 [8192, 256], P(('row', 'rep'))
- grad_self: float32 [256, 256], replicated
- grad_neigh: float32 [256, 256], replicated
- grad_features: bfloat16 [8192, 256], P(('row', 'rep'))
Inputs may be any that keep to these rules, and one draw needn't show every extreme that they name: `tile_count`: for some row index and section all 48 slots are live in every draw.
All inputs are finite; a program needn't handle non-finite values.
Results may differ from a plain program's by a relative error of at most 0.024.
Values may be sent and summed in bfloat16 or wider, within the bound.
A program may use at most 64 MiB of HBM per device.

v0:
```python
import jax
import jax.numpy as jnp
from jax import lax
from jax.sharding import PartitionSpec as P


def from_root(value, axis, source):
    kept = jnp.where(lax.axis_index(axis) == source, value, 0).astype(value.dtype)
    return lax.psum(kept, axis)


def hot_tables(blocks, count, nblk, slots):
    live = (jnp.arange(slots) < count).astype(jnp.float32)
    dest_hot = (blocks[:, 0][:, None] == jnp.arange(nblk)[None, :]).astype(jnp.float32) * live[
        :, None
    ]
    src_hot = (blocks[:, 1][:, None] == jnp.arange(nblk)[None, :]).astype(jnp.float32)
    return (dest_hot, src_hot)


def body(
    features, weight_self, weight_neigh, degrees, tile_values, tile_blocks, tile_count, cotangent
):
    rows, width = features.shape
    tile = tile_values.shape[3]
    slots = tile_values.shape[2]
    sections_here = tile_values.shape[1]
    nblk = rows // tile
    nrep = lax.axis_size("rep")
    share = rows // nrep
    rep_pos = lax.axis_index("rep")
    row_pos = lax.axis_index("row")
    partial_value = jnp.zeros((nblk, tile, width), jnp.float32)
    for section in range(sections_here):
        source = from_root(features, "row", rep_pos * sections_here + section)
        source_blocks = source.reshape(nblk, tile, width)
        dest_hot, src_hot = hot_tables(tile_blocks[0, section], tile_count[0, section], nblk, slots)
        picked = jnp.einsum(
            "tc,cif->tif",
            src_hot.astype(jnp.bfloat16),
            source_blocks,
            preferred_element_type=jnp.bfloat16,
        )
        prod = jnp.einsum(
            "tij,tjf->tif", tile_values[0, section], picked, preferred_element_type=jnp.float32
        )
        partial_value = partial_value + jnp.einsum("tb,tif->bif", dest_hot, prod)
    partial_value = partial_value.reshape(rows, width)
    degree_all = degrees.astype(jnp.float32)[:, None]
    degree_mine = lax.dynamic_slice_in_dim(degree_all, rep_pos * share, share, 0)
    feat_mine = lax.dynamic_slice_in_dim(features, rep_pos * share, share, 0)
    agg_part = lax.psum_scatter(partial_value, "rep", scatter_dimension=0, tiled=True)
    agg_mine = (agg_part / degree_mine).astype(jnp.bfloat16)
    pre = jnp.dot(feat_mine, weight_self, preferred_element_type=jnp.float32) + jnp.dot(
        agg_mine, weight_neigh, preferred_element_type=jnp.float32
    )
    sig = jax.nn.sigmoid(pre)
    gpre_mine = (cotangent.astype(jnp.float32) * sig * (1.0 + pre * (1.0 - sig))).astype(
        jnp.bfloat16
    )
    dagg_mine = (
        jnp.dot(gpre_mine, weight_neigh.T, preferred_element_type=jnp.float32) / degree_mine
    ).astype(jnp.bfloat16)
    dagg_all = lax.all_gather(dagg_mine, "rep", axis=0, tiled=True)
    output = jax.nn.silu(pre).astype(jnp.bfloat16)
    grad_self_part = jnp.dot(feat_mine.T, gpre_mine, preferred_element_type=jnp.float32)
    grad_neigh_part = jnp.dot(agg_mine.T, gpre_mine, preferred_element_type=jnp.float32)
    grad_self, grad_neigh = lax.psum((grad_self_part, grad_neigh_part), ("row", "rep"))
    dagg_blocks = dagg_all.reshape(nblk, tile, width)
    terms = []
    for section in range(sections_here):
        dest_hot, src_hot = hot_tables(tile_blocks[0, section], tile_count[0, section], nblk, slots)
        picked = jnp.einsum(
            "tb,bif->tif",
            dest_hot.astype(jnp.bfloat16),
            dagg_blocks,
            preferred_element_type=jnp.bfloat16,
        )
        contrib = jnp.einsum(
            "tij,tif->tjf", tile_values[0, section], picked, preferred_element_type=jnp.float32
        )
        terms.append(jnp.einsum("tc,tjf->cjf", src_hot, contrib).reshape(rows, width))
    stacked = jnp.stack(terms, 0)
    summed = lax.psum(stacked, "row")
    owned = lax.dynamic_index_in_dim(summed, row_pos % sections_here, 0, keepdims=False).astype(
        jnp.bfloat16
    )
    everyone = from_root(owned, "rep", row_pos // sections_here)
    back_mine = lax.dynamic_slice_in_dim(everyone, rep_pos * share, share, 0)
    grad_features = (
        jnp.dot(gpre_mine, weight_self.T, preferred_element_type=jnp.float32)
        + back_mine.astype(jnp.float32)
    ).astype(jnp.bfloat16)
    return (output, grad_self, grad_neigh, grad_features)


def solution(mesh):
    in_specs = (
        P("row", None),
        P(),
        P(),
        P("row"),
        P("row", "rep", None, None, None),
        P("row", "rep", None, None),
        P("row", "rep"),
        P(("row", "rep"), None),
    )
    out_specs = (P(("row", "rep"), None), P(), P(), P(("row", "rep"), None))
    return jax.shard_map(body, mesh=mesh, in_specs=in_specs, out_specs=out_specs, check_vma=False)
```

profile of v0, /device:TPU:0, one launch (start us, length us, event | category | flops | bytes accessed | tf_op | source)
XLA Modules:
  0.0 399.4 jit_solution(14081113110862203722)
XLA Ops:
  7.2 2.3 broadcast_select_fusion.1
  13.0 57.8 %all-reduce.11.cloned.1.call-done = (bf16[8,128,256]{2,1,0:T(8,128)(2,1)}, bf16[8,128,256]{2,1,0:T(8,128)(2,1)}) async-done(((bf16[8,128,256]{2,1,0:T(8,128)(2,1)}, bf16[8,128,256]{2,1,0:T(8,128)(2,1)}), (bf16[8,128,256]{2,1,0:T(8,128)(2,1)}, bf16[8,128,256]{2,1,0:T(8,128)(2,1)})) %all-reduce.11.cloned.1.call-update) | async-done | bytes 1048592 | tf_op jit(solution)/shard_map/psum | solution.py:9
  70.7 2.1 fusion.31
  72.8 3.3 fusion.12
  76.0 3.8 copy.22
  79.9 2.2 fusion.33
  82.1 3.2 fusion.14
  85.3 4.9 %copy.19 = bf16[48,256,128]{1,0,2:T(8,128)(2,1)} copy(bf16[48,256,128]{2,1,0:T(8,128)(2,1)} %fusion.14) | data formatting | bytes 6291456 | tf_op jit(solution)/shard_map/tij,tjf->tif/dot_general | solution.py:44
  95.3 25.4 %reduce-scatter.2.cloned.1.call-done = f32[256,256]{1,0:T(8,128)} async-done(((f32[1024,256]{1,0:T(8,128)}), f32[256,256]{1,0:T(8,128)}) %reduce-scatter.2.cloned.1.call-update) | async-done | bytes 262160 | tf_op jit(solution)/shard_map/reduce_scatter | solution.py:52
  120.7 1.9 multiply_convert_fusion
  122.9 16.2 %all_gather.3 = bf16[1024,256]{1,0:T(8,128)(2,1)S(1)} all-gather(bf16[256,256]{1,0:T(8,128)(2,1)S(1)} %fusion.28), channel_id=1, replica_groups=mesh['row'=8,'rep'=4] {'rep'}, dimensions={0}, use_global_device_ids=true | all-gather | bytes 655360 | tf_op jit(solution)/shard_map/all_gather | solution.py:64
  140.1 2.7 fusion.35
  142.8 3.1 fusion.10
  145.9 3.8 copy.25
  153.0 3.1 fusion.8
  156.1 3.8 copy.27
  161.3 56.4 %all-reduce.12 = bf16[2,1024,256]{2,1,0:T(8,128)(2,1)S(1)} all-reduce(f32[2,1024,256]{2,1,0:T(8,128)S(1)} %pad_maximum_fusion), channel_id=1, replica_groups=mesh['row'=8,'rep'=4] {'row'}, use_global_device_ids=true, to_apply=%region_5.6 | all-reduce | flops 524288 | bytes 3145728 | tf_op jit(solution)/shard_map/psum | solution.py:84
  218.6 1.8 fusion.39
  220.4 2.0 fusion.77
  222.4 32.1 %all-reduce.7.cloned.1.call-done = bf16[1024,256]{1,0:T(8,128)(2,1)} async-done(((bf16[1024,256]{1,0:T(8,128)(2,1)}), bf16[1024,256]{1,0:T(8,128)(2,1)}) %all-reduce.7.cloned.1.call-update) | async-done | bytes 524304 | tf_op jit(solution)/shard_map/psum | solution.py:9
  254.5 1.8 fusion.27
  256.3 133.3 %all-reduce.9.cloned.1.call-done = (f32[256,256]{1,0:T(8,128)}, f32[256,256]{1,0:T(8,128)}) async-done(((f32[256,256]{1,0:T(8,128)}, f32[256,256]{1,0:T(8,128)}), (f32[256,256]{1,0:T(8,128)}, f32[256,256]{1,0:T(8,128)})) %all-reduce.9.cloned.1.call-update) | async-done | bytes 524304 | tf_op jit(solution)/shard_map/psum | solution.py:68
  389.6 1.7 copy.51
  391.2 1.7 copy.52
  (61 shorter events, 15.1 us)
Async XLA Ops:
  7.2 113.6 %copy-start = (bf16[256,256]{1,0:T(8,128)(2,1)S(1)}, bf16[256,256]{1,0:T(8,128)(2,1)}, u32[]{:S(2)}) copy-start(bf16[256,256]{1,0:T(8,128)(2,1)} %param.10) | copy-start | bytes 393220
  7.2 63.5 %all-reduce.11.cloned.1.call-start = ((), (), s32[]{:S(2)}) async-start(), calls=%async_computation.4 | async-start | bytes 2097152 | tf_op jit(solution)/shard_map/psum | solution.py:9
  7.2 65.5 %copy-start.3 = (bf16[1,2,48,128,128]{4,3,2,1,0:T(8,128)(2,1)S(1)}, bf16[1,2,48,128,128]{4,3,2,1,0:T(8,128)(2,1)}, u32[]{:S(2)}) copy-start(bf16[1,2,48,128,128]{4,3,2,1,0:T(8,128)(2,1)} %param.12) | copy-start | bytes 9437188
  9.5 111.2 %reduce-scatter.2.cloned.1.call-start = ((), (), s32[]{:S(2)}) async-start(), calls=%async_computation.1 | async-start | bytes 1310720 | tf_op jit(solution)/shard_map/reduce_scatter | solution.py:52
  11.6 78.7 %copy-start.10 = (bf16[48]{0:T(256)(128)(2,1)}, bf16[48]{0:T(256)(128)(2,1)S(1)}, u32[]{:S(2)}) copy-start(bf16[48]{0:T(256)(128)(2,1)S(1)} %compare_convert_fusion) | copy-start | bytes 292
  12.2 78.5 %copy-start.12 = (bf16[48]{0:T(256)(128)(2,1)}, bf16[48]{0:T(256)(128)(2,1)S(1)}, u32[]{:S(2)}) copy-start(bf16[48]{0:T(256)(128)(2,1)S(1)} %compare_convert_fusion.1) | copy-start | bytes 292
  79.9 2.2 copy-start.4
  90.2 1.9 copy-start.1
  92.1 1.9 copy-start.9
  92.1 2.1 copy-start.8
  92.7 28.1 %copy-start.16 = (bf16[256,256]{1,0:T(8,128)(2,1)S(1)}, bf16[256,256]{1,0:T(8,128)(2,1)}, u32[]{:S(2)}) copy-start(bf16[256,256]{1,0:T(8,128)(2,1)} %param.15) | copy-start | bytes 393220
  94.0 45.1 %copy-start.13 = (bf16[48]{0:T(256)(128)(2,1)S(1)}, bf16[48]{0:T(256)(128)(2,1)}, u32[]{:S(2)}) copy-start(bf16[48]{0:T(256)(128)(2,1)} %copy-done.12) | copy-start | bytes 292
  94.0 160.5 %all-reduce.7.cloned.1.call-start = ((), (), s32[]{:S(2)}) async-start(), calls=%async_computation.2 | async-start | bytes 1048576 | tf_op jit(solution)/shard_map/psum | solution.py:9
  94.2 45.9 %copy-start.14 = (f32[256]{0:T(256)}, f32[256]{0:T(256)S(1)}, u32[]{:S(2)}) copy-start(f32[256]{0:T(256)S(1)} %dynamic-slice.3) | copy-start | bytes 3076
  122.7 17.5 %copy-start.11 = (bf16[48]{0:T(256)(128)(2,1)S(1)}, bf16[48]{0:T(256)(128)(2,1)}, u32[]{:S(2)}) copy-start(bf16[48]{0:T(256)(128)(2,1)} %copy-done.10) | copy-start | bytes 292
  139.1 3.7 copy-start.5
  149.8 2.1 copy-start.2
  149.8 3.2 copy-start.6
  159.9 1.2 copy-start.7
  161.3 59.1 %copy-start.15 = (f32[256]{0:T(256)S(1)}, f32[256]{0:T(256)}, u32[]{:S(2)}) copy-start(f32[256]{0:T(256)} %copy-done.14) | copy-start | bytes 3076
  218.5 171.0 %all-reduce.9.cloned.1.call-start = ((), (), s32[]{:S(2)}) async-start(), calls=%async_computation.3 | async-start | bytes 1048576 | tf_op jit(solution)/shard_map/psum | solution.py:68
Sparse Core Ops, SparseCore 0:
  11.2 59.4 all-reduce.10
  94.1 26.5 reduce-scatter.1
  218.7 35.8 all-reduce.6
  260.4 129.1 all-reduce.8
where the time goes:
time: 400 us; the launch traced here: 399 us
  waiting for transfers between devices  249 us (62%)
  blocking collectives  72.6 us (18%)
  matrix products  31.5 us (8%)
  local copies, waits for them, and re-layouts  28 us (7%)
  between operations  14 us (4%)
  other arithmetic  4.54 us (1%)
    psum x1, waiting for transfers between devices, body(): lax.psum((grad_self_part, grad_neigh_part), ('row', 'rep'))  133 us
    psum x2, waiting for transfers between devices, from_root(): return lax.psum(kept, axis)  89.8 us
    psum x1, blocking collectives, body(): summed = lax.psum(stacked, 'row')  56.4 us
    reduce_scatter x1, waiting for transfers between devices, body(): lax.psum_scatter(partial_value, 'rep', scatter_dimension=0, tiled=True)  25.4 us
    all_gather x1, blocking collectives, body(): dagg_all = lax.all_gather(dagg_mine, 'rep', axis=0, tiled=True)  16.2 us
    dot_general x2, local copies, waits for them, and re-layouts, body(): jnp.einsum('tij,tjf->tif', tile_values[0, section], picked, preferred_ele...  8.77 us
  transfers between devices with their start and end apart: 4, of which 4 were waited for; matrix products, arithmetic and copies ran while one was open for 3% of the time, Pallas kernels for 0%

commit v1 on v0

--- a/solution.py
+++ b/solution.py
@@ -65,7 +65,9 @@
     output = jax.nn.silu(pre).astype(jnp.bfloat16)
     grad_self_part = jnp.dot(feat_mine.T, gpre_mine, preferred_element_type=jnp.float32)
     grad_neigh_part = jnp.dot(agg_mine.T, gpre_mine, preferred_element_type=jnp.float32)
-    grad_self, grad_neigh = lax.psum((grad_self_part, grad_neigh_part), ("row", "rep"))
+    grad_self, grad_neigh = lax.psum(
+        lax.psum((grad_self_part, grad_neigh_part), axis_name="rep"), axis_name="row"
+    )
     dagg_blocks = dagg_all.reshape(nblk, tile, width)
     terms = []
     for section in range(sections_here):

time: 400 us -> 326 us (0.81)
  waiting for transfers between devices: 249 us -> 176 us
    psum x1 -> x2, waiting for transfers between devices: 133 us -> 55.9 us  [the longest x1 55.9 us: body(): lax.psum(lax.psum((grad_self_part, grad_neigh_part), axis_name='rep'), ax...]
  transfers between devices with their start and end apart: 4 -> 5, of which waited for: 4 -> 4; matrix products, arithmetic and copies ran while one was open for 3% -> 2% of each run, Pallas kernels for 0% -> 0%
where the time goes in v1:
time: 326 us; the launch traced here: 325 us
  waiting for transfers between devices  176 us (54%)
  blocking collectives  73.4 us (23%)
  matrix products  28.7 us (9%)
  local copies, waits for them, and re-layouts  28.3 us (9%)
  between operations  14.1 us (4%)
  other arithmetic  4.58 us (1%)
    psum x2, waiting for transfers between devices, from_root(): return lax.psum(kept, axis)  93 us
    psum x1, blocking collectives, body(): summed = lax.psum(stacked, 'row')  57.3 us
    psum x1, waiting for transfers between devices, body(): lax.psum(lax.psum((grad_self_part, grad_neigh_part), axis_name='rep'), ax...  55.9 us
    reduce_scatter x1, waiting for transfers between devices, body(): lax.psum_scatter(partial_value, 'rep', scatter_dimension=0, tiled=True)  26.3 us
    all_gather x1, blocking collectives, body(): dagg_all = lax.all_gather(dagg_mine, 'rep', axis=0, tiled=True)  16.2 us
    dot_general x2, local copies, waits for them, and re-layouts, body(): jnp.einsum('tij,tjf->tif', tile_values[0, section], picked, preferred_ele...  8.8 us
    dot_general x2, local copies, waits for them, and re-layouts, body(): jnp.einsum('tij,tif->tjf', tile_values[0, section], picked, preferred_ele...  7.7 us
    unnamed x40, local copies, waits for them, and re-layouts  6.74 us
  transfers between devices with their start and end apart: 5, of which 4 were waited for; matrix products, arithmetic and copies ran while one was open for 2% of the time, Pallas kernels for 0%

profile of v1, /device:TPU:0, one launch (start us, length us, event | category | flops | bytes accessed | tf_op | source)
XLA Modules:
  0.0 325.1 jit_solution(15807273443050486945)
XLA Ops:
  7.2 2.3 broadcast_select_fusion.1
  13.0 57.7 %all-reduce.15.cloned.1.call-done = (bf16[8,128,256]{2,1,0:T(8,128)(2,1)}, bf16[8,128,256]{2,1,0:T(8,128)(2,1)}) async-done(((bf16[8,128,256]{2,1,0:T(8,128)(2,1)}, bf16[8,128,256]{2,1,0:T(8,128)(2,1)}), (bf16[8,128,256]{2,1,0:T(8,128)(2,1)}, bf16[8,128,256]{2,1,0:T(8,128)(2,1)})) %all-reduce.15.cloned.1.call-update) | async-done | bytes 1048592 | tf_op jit(solution)/shard_map/psum | solution.py:9
  70.7 2.1 fusion.31
  72.8 3.2 fusion.12
  76.0 3.8 %copy.22 = bf16[48,256,128]{1,0,2:T(8,128)(2,1)S(1)} copy(bf16[48,256,128]{2,1,0:T(8,128)(2,1)} %fusion.12) | data formatting | bytes 6291456 | tf_op jit(solution)/shard_map/tij,tjf->tif/dot_general | solution.py:44
  79.9 2.2 fusion.33
  82.1 3.2 fusion.14
  85.3 5.0 %copy.19 = bf16[48,256,128]{1,0,2:T(8,128)(2,1)} copy(bf16[48,256,128]{2,1,0:T(8,128)(2,1)} %fusion.14) | data formatting | bytes 6291456 | tf_op jit(solution)/shard_map/tij,tjf->tif/dot_general | solution.py:44
  90.8 1.4 copy-done.1
  92.7 1.3 copy.14
  94.4 26.3 %reduce-scatter.2.cloned.1.call-done = f32[256,256]{1,0:T(8,128)} async-done(((f32[1024,256]{1,0:T(8,128)}), f32[256,256]{1,0:T(8,128)}) %reduce-scatter.2.cloned.1.call-update) | async-done | bytes 262160 | tf_op jit(solution)/shard_map/reduce_scatter | solution.py:52
  120.8 1.9 multiply_convert_fusion
  122.9 16.2 %all_gather.3 = bf16[1024,256]{1,0:T(8,128)(2,1)S(1)} all-gather(bf16[256,256]{1,0:T(8,128)(2,1)S(1)} %fusion.28), channel_id=1, replica_groups=mesh['row'=8,'rep'=4] {'rep'}, dimensions={0}, use_global_device_ids=true | all-gather | bytes 655360 | tf_op jit(solution)/shard_map/all_gather | solution.py:64
  140.2 2.6 fusion.35
  143.7 3.1 fusion.10
  146.8 3.8 %copy.25 = bf16[48,256,128]{1,0,2:T(8,128)(2,1)S(1)} copy(bf16[48,256,128]{2,1,0:T(8,128)(2,1)} %fusion.10) | data formatting | bytes 6291456 | tf_op jit(solution)/shard_map/tij,tif->tjf/dot_general | solution.py:81
  153.9 3.1 fusion.8
  157.0 3.8 %copy.27 = bf16[48,256,128]{1,0,2:T(8,128)(2,1)S(1)} copy(bf16[48,256,128]{2,1,0:T(8,128)(2,1)} %fusion.8) | data formatting | bytes 6291456 | tf_op jit(solution)/shard_map/tij,tif->tjf/dot_general | solution.py:81
  163.5 57.3 %all-reduce.16 = bf16[2,1024,256]{2,1,0:T(8,128)(2,1)S(1)} all-reduce(f32[2,1024,256]{2,1,0:T(8,128)S(1)} %pad_maximum_fusion), channel_id=1, replica_groups=mesh['row'=8,'rep'=4] {'row'}, use_global_device_ids=true, to_apply=%region_7.8 | all-reduce | flops 524288 | bytes 3145728 | tf_op jit(solution)/shard_map/psum | solution.py:86
  222.3 35.3 %all-reduce.9.cloned.1.call-done = bf16[1024,256]{1,0:T(8,128)(2,1)} async-done(((bf16[1024,256]{1,0:T(8,128)(2,1)}), bf16[1024,256]{1,0:T(8,128)(2,1)}) %all-reduce.9.cloned.1.call-update) | async-done | bytes 524304 | tf_op jit(solution)/shard_map/psum | solution.py:9
  257.5 1.8 fusion.27
  259.3 55.9 %all-reduce.11.cloned.1.call-done = (f32[256,256]{1,0:T(8,128)}, f32[256,256]{1,0:T(8,128)}) async-done(((f32[256,256]{1,0:T(8,128)}, f32[256,256]{1,0:T(8,128)}), (f32[256,256]{1,0:T(8,128)}, f32[256,256]{1,0:T(8,128)})) %all-reduce.11.cloned.1.call-update) | async-done | bytes 524304 | tf_op jit(solution)/shard_map/psum | solution.py:68
  315.2 1.7 copy.53
  316.9 1.7 copy.54
  (68 shorter events, 14.3 us)
Async XLA Ops:
  7.2 113.6 %copy-start = (bf16[256,256]{1,0:T(8,128)(2,1)S(1)}, bf16[256,256]{1,0:T(8,128)(2,1)}, u32[]{:S(2)}) copy-start(bf16[256,256]{1,0:T(8,128)(2,1)} %param.10) | copy-start | bytes 393220
  7.2 63.5 %all-reduce.15.cloned.1.call-start = ((), (), s32[]{:S(2)}) async-start(), calls=%async_computation.5 | async-start | bytes 2097152 | tf_op jit(solution)/shard_map/psum | solution.py:9
  7.2 65.5 %copy-start.3 = (bf16[1,2,48,128,128]{4,3,2,1,0:T(8,128)(2,1)S(1)}, bf16[1,2,48,128,128]{4,3,2,1,0:T(8,128)(2,1)}, u32[]{:S(2)}) copy-start(bf16[1,2,48,128,128]{4,3,2,1,0:T(8,128)(2,1)} %param.12) | copy-start | bytes 9437188
  9.6 111.2 %reduce-scatter.2.cloned.1.call-start = ((), (), s32[]{:S(2)}) async-start(), calls=%async_computation.1 | async-start | bytes 1310720 | tf_op jit(solution)/shard_map/reduce_scatter | solution.py:52
  11.6 78.7 %copy-start.11 = (bf16[48]{0:T(256)(128)(2,1)}, bf16[48]{0:T(256)(128)(2,1)S(1)}, u32[]{:S(2)}) copy-start(bf16[48]{0:T(256)(128)(2,1)S(1)} %compare_convert_fusion) | copy-start | bytes 292
  12.2 78.5 %copy-start.13 = (bf16[48]{0:T(256)(128)(2,1)}, bf16[48]{0:T(256)(128)(2,1)S(1)}, u32[]{:S(2)}) copy-start(bf16[48]{0:T(256)(128)(2,1)S(1)} %compare_convert_fusion.1) | copy-start | bytes 292
  79.9 2.2 copy-start.4
  90.3 1.9 copy-start.1
  92.1 2.0 copy-start.10
  92.2 2.1 copy-start.8
  92.2 2.1 copy-start.9
  92.7 28.1 %copy-start.18 = (bf16[256,256]{1,0:T(8,128)(2,1)S(1)}, bf16[256,256]{1,0:T(8,128)(2,1)}, u32[]{:S(2)}) copy-start(bf16[256,256]{1,0:T(8,128)(2,1)} %param.15) | copy-start | bytes 393220
  94.0 45.1 %copy-start.14 = (bf16[48]{0:T(256)(128)(2,1)S(1)}, bf16[48]{0:T(256)(128)(2,1)}, u32[]{:S(2)}) copy-start(bf16[48]{0:T(256)(128)(2,1)} %copy-done.13) | copy-start | bytes 292
  94.0 127.7 %all-reduce.13.cloned.1.call-start = ((), (), s32[]{:S(2)}) async-start(), calls=%async_computation.4 | async-start | bytes 1048576 | tf_op jit(solution)/shard_map/psum | solution.py:69
  94.2 45.9 %copy-start.15 = (f32[256]{0:T(256)}, f32[256]{0:T(256)S(1)}, u32[]{:S(2)}) copy-start(f32[256]{0:T(256)S(1)} %dynamic-slice.3) | copy-start | bytes 3076
  122.7 17.4 %copy-start.12 = (bf16[48]{0:T(256)(128)(2,1)S(1)}, bf16[48]{0:T(256)(128)(2,1)}, u32[]{:S(2)}) copy-start(bf16[48]{0:T(256)(128)(2,1)} %copy-done.11) | copy-start | bytes 292
  139.1 4.6 %copy-start.5 = (bf16[1,2,48,128,128]{4,3,2,1,0:T(8,128)(2,1)S(1)}, bf16[1,2,48,128,128]{4,3,2,1,0:T(8,128)(2,1)}, u32[]{:S(2)}) copy-start(bf16[1,2,48,128,128]{4,3,2,1,0:T(8,128)(2,1)} %param.12) | copy-start | bytes 9437188
  150.7 2.1 copy-start.2
  150.7 3.2 copy-start.6
  160.9 1.2 copy-start.7
  161.4 0.8 copy-start.16
  161.4 1.0 copy-start.17
  163.5 94.1 %all-reduce.9.cloned.1.call-start = ((), (), s32[]{:S(2)}) async-start(), calls=%async_computation.2 | async-start | bytes 1048576 | tf_op jit(solution)/shard_map/psum | solution.py:9
  221.7 93.6 %all-reduce.11.cloned.1.call-start = ((), (), s32[]{:S(2)}) async-start(), calls=%async_computation.3 | async-start | bytes 1048576 | tf_op jit(solution)/shard_map/psum | solution.py:68
Sparse Core Ops, SparseCore 0:
  11.2 59.4 all-reduce.14
  94.2 26.5 reduce-scatter.1
  163.6 36.9 all-reduce.12
  221.8 35.7 all-reduce.8
  260.5 54.6 all-reduce.10
